TPU v7x, 32 devices: a whole 2x2x4 slice. The times are simulated.
32 devices in a mesh: dp: 4 (over z), expert: 8 (over y, x, core).
Axes of the slice: x: 2, y: 2, z: 4, core: 2. Of those that a mesh axis runs over, the one named last changes fastest.
Arguments:
- out_grad: bfloat16 [8192, 4096], P(('dp', 'expert')), may hold values from -6 to 6
- destination: int32 [8192, 1], P(('dp', 'expert')), may hold values from 0 to 7; in each aligned block of 256 rows (0 to 255, 256 to 511, ...) at most 64 rows name the same one
- hidden: bfloat16 [16384, 1024], P(('dp', 'expert')), may hold values from -6 to 6
- weight: bfloat16 [8, 1024, 4096], P('expert', None, 'dp'), may hold values from -0.09375 to 0.09375
- left_prev: float32 [8, 2048, 1024], P('expert', 'dp'), may hold values from -3 to 3
- right_prev: float32 [8, 4096, 2048], P('expert', 'dp'), may hold values from -3 to 3
Outputs:
- grad_rows: bfloat16 [8192, 1024], P(('dp', 'expert'))
- left_stats: float32 [8, 2048, 1024], P('expert', 'dp')
- right_stats: float32 [8, 4096, 2048], P('expert', 'dp')
Inputs may be any that keep to these rules, and one draw needn't show every extreme that they name: Among the rows of one device at most 64 have the same destination, and on some device that many do.
All inputs are finite; a program needn't handle non-finite values.
Results may differ from a plain program's by a relative error of at most 0.001.
Values may be sent and summed in bfloat16 or wider, within the bound.
A program may use at most 128 MiB of HBM per device.

v0:
```python
import jax
import jax.numpy as jnp
from jax import lax
from jax.sharding import PartitionSpec as P

ema_decay = 0.9


def swapped(value, axis, distance):
    mask = 2**distance
    pairs = [(source, source ^ mask) for source in range(lax.axis_size(axis))]
    return lax.ppermute(value, axis, pairs)


def slot_places(dest_column, expert_count, capacity):
    choose = (dest_column[:, None] == jnp.arange(expert_count, dtype=jnp.int32)[None, :]).astype(
        jnp.int32
    )
    before = jnp.cumsum(choose, axis=0) - choose
    slot_rank = jnp.sum(before * choose, axis=1)
    return dest_column * capacity + slot_rank


def local(out_grad, destination, hidden, weight, left_prev, right_prev):
    expert_count = lax.axis_size("expert")
    group_count = lax.axis_size("dp")
    row_count, model_width = out_grad.shape
    slot_count, hidden_width = hidden.shape
    capacity = slot_count // expert_count
    target_slots = slot_places(destination[:, 0], expert_count, capacity)
    outgoing = jnp.zeros((slot_count, model_width), out_grad.dtype).at[target_slots].set(out_grad)
    arrived = lax.all_to_all(
        outgoing.reshape(expert_count, capacity, model_width),
        "expert",
        split_axis=0,
        concat_axis=0,
        tiled=True,
    )
    arrived = arrived.reshape(slot_count, model_width)
    columns = arrived
    slot_grad = lax.dot_general(
        columns,
        lax.all_gather(weight[0], "dp", axis=1, tiled=True),
        (((1,), (1,)), ((), ())),
        preferred_element_type=jnp.float32,
    ).astype(jnp.bfloat16)
    returned = lax.all_to_all(
        slot_grad.reshape(expert_count, capacity, hidden_width),
        "expert",
        split_axis=0,
        concat_axis=0,
        tiled=True,
    )
    grad_rows = returned.reshape(slot_count, hidden_width)[target_slots]
    half_width = model_width // group_count
    block_width = 2 * half_width
    columns_all = lax.all_to_all(arrived, "dp", split_axis=1, concat_axis=0, tiled=True)
    columns = columns_all
    own_piece = lax.dot_general(
        columns,
        lax.all_gather(hidden, "dp", axis=0, tiled=True),
        (((0,), (0,)), ((), ())),
        preferred_element_type=jnp.float32,
    )
    partner = swapped(own_piece.astype(jnp.bfloat16), "dp", 0).astype(own_piece.dtype)
    parity = lax.axis_index("dp") % 2
    upper_half = parity == 0
    first_half = jnp.where(upper_half, own_piece, partner)
    second_half = jnp.where(upper_half, partner, own_piece)
    block_grad = jnp.concatenate([first_half, second_half], axis=0)
    scale_left = 1.0 / (group_count * row_count * block_width)
    scale_right = 1.0 / (group_count * row_count * hidden_width)
    right_gram = (
        lax.dot_general(
            own_piece,
            block_grad,
            (((1,), (1,)), ((), ())),
            precision=lax.Precision.HIGHEST,
            preferred_element_type=jnp.float32,
        )
        * scale_right
    )
    half_hidden = hidden_width // 2
    hidden_cols = lax.dynamic_slice_in_dim(block_grad, parity * half_hidden, half_hidden, 1)
    left_gram = (
        lax.dot_general(
            hidden_cols,
            block_grad,
            (((0,), (0,)), ((), ())),
            precision=lax.Precision.HIGHEST,
            preferred_element_type=jnp.float32,
        )
        * scale_left
    )
    left_stats = ema_decay * left_prev + (1.0 - ema_decay) * left_gram[None]
    right_stats = ema_decay * right_prev + (1.0 - ema_decay) * right_gram[None]
    return (grad_rows, left_stats, right_stats)


def solution(mesh):
    placed = (
        P(("dp", "expert"), None),
        P(("dp", "expert"), None),
        P(("dp", "expert"), None),
        P("expert", None, "dp"),
        P("expert", "dp", None),
        P("expert", "dp", None),
    )
    return jax.shard_map(
        local,
        mesh=mesh,
        in_specs=placed,
        out_specs=(P(("dp", "expert"), None), P("expert", "dp", None), P("expert", "dp", None)),
        check_vma=False,
    )
```

profile of v0, /device:TPU:1, one launch (start us, length us, event | category | flops | bytes accessed | tf_op | source)
XLA Modules:
  0.0 439.9 jit_solution(14873368726343647602)
XLA Ops:
  7.2 0.0 all-gather.4.cloned.1.call-start
  7.2 0.7 all-gather.4.cloned.1.call-update
  7.9 0.7 fusion.15
  8.6 0.6 reduce-window.6
  9.2 0.2 slice_reduce_fusion
  9.4 0.8 fusion.14
  10.2 0.7 compare_select_fusion
  10.9 7.1 %scatter_custom_fusion = bf16[512,4096]{1,0:T(8,128)(2,1)} fusion(s32[256]{0:T(256)S(1)} %bitcast.37, bf16[256,4096]{1,0:T(8,128)(2,1)} %param.6, bf16[]{:T(256)} %constant.14.clone.1), kind=kCustom, calls=%fused_computation.14 | custom fusion | bytes 4194816 | tf_op jit(solution)/shard_map/scatter | solution.py:31
  18.0 5.2 %all-to-all-start = ((bf16[8,64,4096]{2,1,0:T(8,128)(2,1)}), bf16[8,64,4096]{2,1,0:T(8,128)(2,1)}, u32[]{:S(2)}, u32[]{:S(2)}) async-start(bf16[8,64,4096]{2,1,0:T(8,128)(2,1)} %bitcast.34), calls=%async_computation | async-start | bytes 8388608 | tf_op jit(solution)/shard_map/all_to_all | solution.py:32
  23.2 0.0 all-gather.6.cloned.1.call-start
  23.2 0.7 all-gather.6.cloned.1.call-update
  23.9 44.9 %all-to-all-done = bf16[8,64,4096]{2,1,0:T(8,128)(2,1)} async-done(((bf16[8,64,4096]{2,1,0:T(8,128)(2,1)}), bf16[8,64,4096]{2,1,0:T(8,128)(2,1)}, u32[]{:S(2)}, u32[]{:S(2)}) %all-to-all-start) | async-done | bytes 4194336 | tf_op jit(solution)/shard_map/all_to_all | solution.py:32
  68.9 7.8 %all_to_all.22 = bf16[512,4,1024]{2,1,0:T(4,128)(2,1)} reshape(bf16[8,64,4096]{2,1,0:T(8,128)(2,1)} %all-to-all-done) | data formatting | bytes 8388608 | tf_op jit(solution)/shard_map/all_to_all | solution.py:57
  76.7 5.5 %copy.10 = bf16[512,4,1024]{2,0,1:T(8,128)(2,1)} copy(bf16[512,4,1024]{2,1,0:T(4,128)(2,1)} %all_to_all.22) | data formatting | bytes 8388608 | tf_op jit(solution)/shard_map/all_to_all | solution.py:57
  82.2 5.8 %all-to-all-start.2 = ((bf16[512,4,1024]{2,0,1:T(8,128)(2,1)}), bf16[512,4,1024]{2,0,1:T(8,128)(2,1)}, u32[]{:S(2)}, u32[]{:S(2)}) async-start(bf16[512,4,1024]{2,0,1:T(8,128)(2,1)} %copy.10), calls=%async_computation.2 | async-start | bytes 8388608 | tf_op jit(solution)/shard_map/all_to_all | solution.py:57
  88.0 4.2 all-gather.4.cloned.1.call-done
  92.2 194.6 %all-to-all-done.2 = bf16[512,4,1024]{2,0,1:T(8,128)(2,1)} async-done(((bf16[512,4,1024]{2,0,1:T(8,128)(2,1)}), bf16[512,4,1024]{2,0,1:T(8,128)(2,1)}, u32[]{:S(2)}, u32[]{:S(2)}) %all-to-all-start.2) | async-done | bytes 4194336 | tf_op jit(solution)/shard_map/all_to_all | solution.py:57
  286.8 10.7 %fusion.19 = (bf16[1024,1024]{1,0:T(8,128)(2,1)}, f32[1024,1024]{1,0:T(8,128)}) fusion(bf16[2048,1024]{1,0:T(8,128)(2,1)} %bitcast.12, bf16[2048,1024]{1,0:T(8,128)(2,1)} %all-gather.4.cloned.1.call-done), kind=kOutput, calls=%fused_computation.29 | convolution fusion | flops 4296015872 | bytes 14680064 | tf_op jit(solution)/shard_map/dot_general | solution.py:59
  297.5 0.0 collective-permute-start
  297.5 60.1 %collective-permute-done = bf16[1024,1024]{1,0:T(8,128)(2,1)S(1)} collective-permute-done((bf16[1024,1024]{1,0:T(8,128)(2,1)}, bf16[1024,1024]{1,0:T(8,128)(2,1)S(1)}, u32[]{:S(2)}, u32[]{:S(2)}) %collective-permute-start) | collective-permute-done | bytes 2097184 | tf_op jit(solution)/shard_map/ppermute | solution.py:12
  357.6 7.0 %convert_select_fusion.1 = (f32[1024,1024]{1,0:T(8,128)}, f32[1024,1024]{1,0:T(8,128)}) fusion(f32[1024,1024]{1,0:T(8,128)} %get-tuple-element.6, bf16[1024,1024]{1,0:T(8,128)(2,1)S(1)} %collective-permute-done, pred[]{:T(512)S(6)} %eq.38), kind=kLoop, calls=%fused_computation.11 | loop fusion | flops 3145728 | bytes 14680065 | tf_op jit(solution)/shard_map/jit(_where)/select_n | solution.py:68
  364.6 10.2 %fusion.8 = bf16[512,1024]{1,0:T(8,128)(2,1)} fusion(bf16[512,4096]{1,0:T(8,128)(2,1)} %bitcast.7, bf16[1,1024,4096]{2,1,0:T(8,128)(2,1)} %all-gather.6.cloned.1.call-done), kind=kOutput, calls=%fused_computation.16 | convolution fusion | flops 4295491584 | bytes 13631488 | tf_op jit(solution)/shard_map/dot_general | solution.py:41
  374.9 7.8 %all-to-all-start.1 = ((bf16[8,64,1024]{2,1,0:T(8,128)(2,1)}), bf16[8,64,1024]{2,1,0:T(8,128)(2,1)S(1)}, u32[]{:S(2)}, u32[]{:S(2)}) async-start(bf16[8,64,1024]{2,1,0:T(8,128)(2,1)} %bitcast.9), calls=%async_computation.1 | async-start | bytes 2097152 | tf_op jit(solution)/shard_map/all_to_all | solution.py:47
  382.7 0.0 copy-start
  382.7 0.0 copy-start.1
  382.7 0.0 copy-start.2
  382.7 33.1 %bitcast_add_fusion = f32[1,1024,2048]{2,1,0:T(8,128)} fusion(f32[1,1024,2048]{2,1,0:T(8,128)} %param.11, f32[1024,1024]{1,0:T(8,128)} %get-tuple-element.6, f32[1024,1024]{1,0:T(8,128)} %get-tuple-element.4, f32[1024,1024]{1,0:T(8,128)} %get-tuple-element.3), kind=kOutput, calls=%fused_computation.5 | convolution fusion | flops 25778192384 | bytes 29360128 | tf_op jit(solution)/shard_map/dot_general | solution.py:74
  415.8 0.0 copy-done
  415.8 0.0 copy-done.1
  415.8 15.1 %bitcast_add_fusion.1 = f32[1,512,1024]{2,1,0:T(8,128)} fusion(f32[1,512,1024]{2,1,0:T(8,128)S(1)} %copy-done.2, f32[1024,1024]{1,0:T(8,128)S(1)} %copy-done.1, f32[1024,1024]{1,0:T(8,128)S(1)} %copy-done, s32[]{:T(128)S(6)} %select_n.32), kind=kOutput, calls=%fused_computation.13 | convolution fusion | flops 12889620480 | bytes 20971524 | tf_op jit(solution)/shard_map/dot_general | solution.py:86
  430.9 0.0 all-to-all-done.1
  430.9 2.0 gather_fusion
  (5 shorter events, 0.1 us)
Async XLA Ops:
  7.2 85.1 %all-gather.4.cloned.1.call-start = ((), (), s32[]{:S(2)}) async-start(), calls=%async_computation.3 | async-start | bytes 5242880 | tf_op jit(solution)/shard_map/all_gather | solution.py:61
  18.0 50.9 %all-to-all-start = ((bf16[8,64,4096]{2,1,0:T(8,128)(2,1)}), bf16[8,64,4096]{2,1,0:T(8,128)(2,1)}, u32[]{:S(2)}, u32[]{:S(2)}) async-start(bf16[8,64,4096]{2,1,0:T(8,128)(2,1)} %bitcast.34), calls=%async_computation | async-start | bytes 8388608 | tf_op jit(solution)/shard_map/all_to_all | solution.py:32
  23.2 341.4 %all-gather.6.cloned.1.call-start = ((), (), s32[]{:S(2)}) async-start(), calls=%async_computation.4 | async-start | bytes 10485760 | tf_op jit(solution)/shard_map/all_gather | solution.py:43
  82.2 204.6 %all-to-all-start.2 = ((bf16[512,4,1024]{2,0,1:T(8,128)(2,1)}), bf16[512,4,1024]{2,0,1:T(8,128)(2,1)}, u32[]{:S(2)}, u32[]{:S(2)}) async-start(bf16[512,4,1024]{2,0,1:T(8,128)(2,1)} %copy.10), calls=%async_computation.2 | async-start | bytes 8388608 | tf_op jit(solution)/shard_map/all_to_all | solution.py:57
  297.5 60.1 %collective-permute-start = (bf16[1024,1024]{1,0:T(8,128)(2,1)}, bf16[1024,1024]{1,0:T(8,128)(2,1)S(1)}, u32[]{:S(2)}, u32[]{:S(2)}) collective-permute-start(bf16[1024,1024]{1,0:T(8,128)(2,1)} %get-tuple-element.5), channel_id=1, source_target_pairs={{0,8},{8,0},{16,24},{24,16},{1,9},{9,1},{17,25},{25,17},{2,10},{10... | collective-permute-start | bytes 6291464 | tf_op jit(solution)/shard_map/ppermute | solution.py:12
  374.9 56.1 %all-to-all-start.1 = ((bf16[8,64,1024]{2,1,0:T(8,128)(2,1)}), bf16[8,64,1024]{2,1,0:T(8,128)(2,1)S(1)}, u32[]{:S(2)}, u32[]{:S(2)}) async-start(bf16[8,64,1024]{2,1,0:T(8,128)(2,1)} %bitcast.9), calls=%async_computation.1 | async-start | bytes 2097152 | tf_op jit(solution)/shard_map/all_to_all | solution.py:47
  382.7 33.1 %copy-start = (f32[1024,1024]{1,0:T(8,128)S(1)}, f32[1024,1024]{1,0:T(8,128)}, u32[]{:S(2)}) copy-start(f32[1024,1024]{1,0:T(8,128)} %get-tuple-element.3) | copy-start | bytes 12582916
  382.7 33.1 %copy-start.1 = (f32[1024,1024]{1,0:T(8,128)S(1)}, f32[1024,1024]{1,0:T(8,128)}, u32[]{:S(2)}) copy-start(f32[1024,1024]{1,0:T(8,128)} %get-tuple-element.4) | copy-start | bytes 12582916
  382.7 33.1 %copy-start.2 = (f32[1,512,1024]{2,1,0:T(8,128)S(1)}, f32[1,512,1024]{2,1,0:T(8,128)}, u32[]{:S(2)}) copy-start(f32[1,512,1024]{2,1,0:T(8,128)} %param.10) | copy-start | bytes 6291460
Sparse Core Ops, SparseCore 0:
  9.5 82.6 all-gather.3
  93.8 223.5 all-gather.5
where the time goes:
time: 446 us; the launch traced here: 440 us
  waiting for transfers between devices  305 us (68%)
  matrix products  69.1 us (15%)
  local copies, waits for them, and re-layouts  22.6 us (5%)
  starting transfers between devices  18.9 us (4%)
  between operations  14.3 us (3%)
  other arithmetic  9.75 us (2%)
    all_to_all x1, waiting for transfers between devices, local(): lax.all_to_all(arrived, 'dp', split_axis=1, concat_axis=0, tiled=True)  195 us
    ppermute x1, waiting for transfers between devices, swapped(): return lax.ppermute(value, axis, pairs)  60.1 us
    all_to_all x1, waiting for transfers between devices, local(): lax.all_to_all(outgoing.reshape(expert_count, capacity, model_width), 'ex...  44.9 us
    dot_general x1, matrix products, local(): lax.dot_general(own_piece, block_grad, (((1,), (1,)), ((), ())), precisio...  33.1 us
    dot_general x1, matrix products, local(): lax.dot_general(hidden_cols, block_grad, (((0,), (0,)), ((), ())), precis...  15.1 us
    all_to_all x2, local copies, waits for them, and re-layouts, local(): lax.all_to_all(arrived, 'dp', split_axis=1, concat_axis=0, tiled=True)  13.3 us
    dot_general x1, matrix products, local(): lax.dot_general(columns, lax.all_gather(hidden, 'dp', axis=0, tiled=True)...  10.7 us
    dot_general x1, matrix products, local(): lax.dot_general(columns, lax.all_gather(weight[0], 'dp', axis=1, tiled=Tr...  10.2 us
  transfers between devices with their start and end apart: 6, of which 4 were waited for; matrix products, arithmetic and copies ran while one was open for 19% of the time, Pallas kernels for 0%

commit v1 on v0

--- a/solution.py
+++ b/solution.py
@@ -1,9 +1,26 @@
+import functools
 import jax
 import jax.numpy as jnp
 from jax import lax
 from jax.sharding import PartitionSpec as P
 
 ema_decay = 0.9
+
+
+def match_corner_up(work_x, ndim_at, k_dim):
+    inter = jnp.concatenate(
+        lax.all_to_all(
+            jnp.stack(jnp.split(work_x, lax.axis_size("dp"), axis=ndim_at)),
+            "dp",
+            split_axis=0,
+            concat_axis=0,
+        ),
+        axis=k_dim,
+    )
+    return inter
+
+
+map_vectors = functools.partial(match_corner_up, ndim_at=1, k_dim=0)
 
 
 def swapped(value, axis, distance):
@@ -54,7 +71,7 @@
     grad_rows = returned.reshape(slot_count, hidden_width)[target_slots]
     half_width = model_width // group_count
     block_width = 2 * half_width
-    columns_all = lax.all_to_all(arrived, "dp", split_axis=1, concat_axis=0, tiled=True)
+    columns_all = map_vectors(arrived)
     columns = columns_all
     own_piece = lax.dot_general(
         columns,

time: 446 us -> 424 us (0.951); the launches traced: 440 us -> 423 us
  local copies, waits for them, and re-layouts: 22.6 us -> 12 us
    all_to_all x1, waiting for transfers between devices: 195 us -> 133 us  [match_corner_up(): lax.all_to_all(jnp.stack(jnp.split(work_x, lax.axis_size('dp'), axis=ndim...]
    all_gather x1, waiting for transfers between devices: 4.23 us -> 39.6 us  [local(): lax.all_gather(hidden, 'dp', axis=0, tiled=True)]
    ppermute x1, waiting for transfers between devices: 60.1 us -> 82.5 us  [swapped(): return lax.ppermute(value, axis, pairs)]
    all_to_all x2 -> x0, local copies, waits for them, and re-layouts: 13.3 us -> none  [local(): lax.all_to_all(arrived, 'dp', split_axis=1, concat_axis=0, tiled=True)]
where the time goes in v1:
time: 424 us; the launch traced here: 423 us
  waiting for transfers between devices  302 us (71%)
  matrix products  68.9 us (16%)
  starting transfers between devices  14.7 us (3%)
  between operations  14.1 us (3%)
  other arithmetic  12.1 us (3%)
  local copies, waits for them, and re-layouts  12 us (3%)
    all_to_all x1, waiting for transfers between devices, match_corner_up(): lax.all_to_all(jnp.stack(jnp.split(work_x, lax.axis_size('dp'), axis=ndim...  133 us
    ppermute x1, waiting for transfers between devices, swapped(): return lax.ppermute(value, axis, pairs)  82.5 us
    all_to_all x1, waiting for transfers between devices, local(): lax.all_to_all(outgoing.reshape(expert_count, capacity, model_width), 'ex...  44.9 us
    all_gather x1, waiting for transfers between devices, local(): lax.all_gather(hidden, 'dp', axis=0, tiled=True)  39.6 us
    dot_general x1, matrix products, local(): lax.dot_general(own_piece, block_grad, (((1,), (1,)), ((), ())), precisio...  32.9 us
    dot_general x1, matrix products, local(): lax.dot_general(hidden_cols, block_grad, (((0,), (0,)), ((), ())), precis...  15.1 us
    dot_general x1, matrix products, local(): lax.dot_general(columns, lax.all_gather(hidden, 'dp', axis=0, tiled=True)...  10.7 us
    dot_general x1, matrix products, local(): lax.dot_general(columns, lax.all_gather(weight[0], 'dp', axis=1, tiled=Tr...  10.2 us
  transfers between devices with their start and end apart: 6, of which 4 were waited for; matrix products, arithmetic and copies ran while one was open for 19% of the time, Pallas kernels for 0%

profile of v1, /device:TPU:1, one launch (start us, length us, event | category | flops | bytes accessed | tf_op | source)
XLA Modules:
  0.0 423.4 jit_solution(742801837169250289)
XLA Ops:
  7.2 0.0 all-gather.4.cloned.1.call-start
  7.2 0.7 all-gather.4.cloned.1.call-update
  7.9 0.7 fusion.15
  8.6 0.6 reduce-window.6
  9.2 0.2 slice_reduce_fusion
  9.4 0.8 fusion.14
  10.2 0.7 compare_select_fusion
  10.9 7.1 %scatter_custom_fusion = bf16[512,4096]{1,0:T(8,128)(2,1)} fusion(s32[256]{0:T(256)S(1)} %bitcast.43, bf16[256,4096]{1,0:T(8,128)(2,1)} %param.6, bf16[]{:T(256)} %constant.14.clone.1), kind=kCustom, calls=%fused_computation.15 | custom fusion | bytes 4194816 | tf_op jit(solution)/shard_map/scatter | solution.py:48
  18.0 5.2 %all-to-all-start = ((bf16[8,64,4096]{2,1,0:T(8,128)(2,1)}), bf16[8,64,4096]{2,1,0:T(8,128)(2,1)}, u32[]{:S(2)}, u32[]{:S(2)}) async-start(bf16[8,64,4096]{2,1,0:T(8,128)(2,1)} %bitcast.40), calls=%async_computation | async-start | bytes 8388608 | tf_op jit(solution)/shard_map/all_to_all | solution.py:49
  23.2 0.0 all-gather.6.cloned.1.call-start
  23.2 0.7 all-gather.6.cloned.1.call-update
  23.9 44.9 %all-to-all-done = bf16[8,64,4096]{2,1,0:T(8,128)(2,1)} async-done(((bf16[8,64,4096]{2,1,0:T(8,128)(2,1)}), bf16[8,64,4096]{2,1,0:T(8,128)(2,1)}, u32[]{:S(2)}, u32[]{:S(2)}) %all-to-all-start) | async-done | bytes 4194336 | tf_op jit(solution)/shard_map/all_to_all | solution.py:49
  68.9 2.6 slice_bitcast_fusion.3
  71.5 2.3 pad_maximum_fusion.3
  73.8 5.3 %all-to-all-start.2 = ((bf16[4,512,1024]{2,1,0:T(8,128)(2,1)}), bf16[4,512,1024]{2,1,0:T(8,128)(2,1)}, u32[]{:S(2)}, u32[]{:S(2)}) async-start(bf16[4,512,1024]{2,1,0:T(8,128)(2,1)} %pad_maximum_fusion.3), calls=%async_computation.2 | async-start | bytes 8388608 | tf_op jit(solution)/shard_map/all_to_all | solution.py:12
  79.1 39.6 %all-gather.4.cloned.1.call-done = bf16[2048,1024]{1,0:T(8,128)(2,1)} async-done(((bf16[512,1024]{1,0:T(8,128)(2,1)}), bf16[2048,1024]{1,0:T(8,128)(2,1)}) %all-gather.4.cloned.1.call-update) | async-done | bytes 4194320 | tf_op jit(solution)/shard_map/all_gather | solution.py:78
  118.8 133.2 %all-to-all-done.2 = bf16[4,512,1024]{2,1,0:T(8,128)(2,1)} async-done(((bf16[4,512,1024]{2,1,0:T(8,128)(2,1)}), bf16[4,512,1024]{2,1,0:T(8,128)(2,1)}, u32[]{:S(2)}, u32[]{:S(2)}) %all-to-all-start.2) | async-done | bytes 4194336 | tf_op jit(solution)/shard_map/all_to_all | solution.py:12
  251.9 10.7 %fusion.19 = (bf16[1024,1024]{1,0:T(8,128)(2,1)}, f32[1024,1024]{1,0:T(8,128)}) fusion(bf16[2048,1024]{1,0:T(8,128)(2,1)} %bitcast.15, bf16[2048,1024]{1,0:T(8,128)(2,1)} %all-gather.4.cloned.1.call-done), kind=kOutput, calls=%fused_computation.34 | convolution fusion | flops 4296015872 | bytes 14680064 | tf_op jit(solution)/shard_map/dot_general | solution.py:76
  262.7 0.0 collective-permute-start
  262.7 82.5 %collective-permute-done = bf16[1024,1024]{1,0:T(8,128)(2,1)S(1)} collective-permute-done((bf16[1024,1024]{1,0:T(8,128)(2,1)}, bf16[1024,1024]{1,0:T(8,128)(2,1)S(1)}, u32[]{:S(2)}, u32[]{:S(2)}) %collective-permute-start) | collective-permute-done | bytes 2097184 | tf_op jit(solution)/shard_map/ppermute | solution.py:29
  345.2 7.0 %convert_select_fusion.1 = (f32[1024,1024]{1,0:T(8,128)}, f32[1024,1024]{1,0:T(8,128)}) fusion(f32[1024,1024]{1,0:T(8,128)} %get-tuple-element.10, bf16[1024,1024]{1,0:T(8,128)(2,1)S(1)} %collective-permute-done, pred[]{:T(512)S(6)} %eq.38), kind=kLoop, calls=%fused_computation.11 | loop fusion | flops 3145728 | bytes 14680065 | tf_op jit(solution)/shard_map/jit(_where)/select_n | solution.py:85
  352.2 0.0 all-gather.6.cloned.1.call-done
  352.2 10.2 %fusion.8 = bf16[512,1024]{1,0:T(8,128)(2,1)} fusion(bf16[512,4096]{1,0:T(8,128)(2,1)} %bitcast.7, bf16[1,1024,4096]{2,1,0:T(8,128)(2,1)} %all-gather.6.cloned.1.call-done), kind=kOutput, calls=%fused_computation.17 | convolution fusion | flops 4295491584 | bytes 13631488 | tf_op jit(solution)/shard_map/dot_general | solution.py:58
  362.5 4.1 all-to-all-start.1
  366.6 0.0 copy-start
  366.6 32.9 %bitcast_add_fusion = f32[1,1024,2048]{2,1,0:T(8,128)} fusion(f32[1,1024,2048]{2,1,0:T(8,128)} %param.11, f32[1024,1024]{1,0:T(8,128)} %get-tuple-element.10, f32[1024,1024]{1,0:T(8,128)} %get-tuple-element.4, f32[1024,1024]{1,0:T(8,128)} %get-tuple-element.3), kind=kOutput, calls=%fused_computation.5 | convolution fusion | flops 25778192384 | bytes 29360128 | tf_op jit(solution)/shard_map/dot_general | solution.py:91
  399.5 0.0 copy-done
  399.5 0.0 copy-done.1
  399.5 0.0 copy-done.2
  399.5 15.1 %bitcast_add_fusion.1 = f32[1,512,1024]{2,1,0:T(8,128)} fusion(f32[1,512,1024]{2,1,0:T(8,128)S(1)} %copy-done.2, f32[1024,1024]{1,0:T(8,128)S(1)} %copy-done.1, f32[1024,1024]{1,0:T(8,128)S(1)} %copy-done, s32[]{:T(128)S(6)} %select_n.32), kind=kOutput, calls=%fused_computation.14 | convolution fusion | flops 12889620480 | bytes 20971524 | tf_op jit(solution)/shard_map/dot_general | solution.py:103
  414.6 0.0 all-to-all-done.1
  414.6 2.0 gather_fusion
  (5 shorter events, 0.1 us)
Async XLA Ops:
  7.2 111.6 %all-gather.4.cloned.1.call-start = ((), (), s32[]{:S(2)}) async-start(), calls=%async_computation.3 | async-start | bytes 5242880 | tf_op jit(solution)/shard_map/all_gather | solution.py:78
  18.0 50.9 %all-to-all-start = ((bf16[8,64,4096]{2,1,0:T(8,128)(2,1)}), bf16[8,64,4096]{2,1,0:T(8,128)(2,1)}, u32[]{:S(2)}, u32[]{:S(2)}) async-start(bf16[8,64,4096]{2,1,0:T(8,128)(2,1)} %bitcast.40), calls=%async_computation | async-start | bytes 8388608 | tf_op jit(solution)/shard_map/all_to_all | solution.py:49
  23.2 329.0 %all-gather.6.cloned.1.call-start = ((), (), s32[]{:S(2)}) async-start(), calls=%async_computation.4 | async-start | bytes 10485760 | tf_op jit(solution)/shard_map/all_gather | solution.py:60
  73.8 178.1 %all-to-all-start.2 = ((bf16[4,512,1024]{2,1,0:T(8,128)(2,1)}), bf16[4,512,1024]{2,1,0:T(8,128)(2,1)}, u32[]{:S(2)}, u32[]{:S(2)}) async-start(bf16[4,512,1024]{2,1,0:T(8,128)(2,1)} %pad_maximum_fusion.3), calls=%async_computation.2 | async-start | bytes 8388608 | tf_op jit(solution)/shard_map/all_to_all | solution.py:12
  262.7 82.5 %collective-permute-start = (bf16[1024,1024]{1,0:T(8,128)(2,1)}, bf16[1024,1024]{1,0:T(8,128)(2,1)S(1)}, u32[]{:S(2)}, u32[]{:S(2)}) collective-permute-start(bf16[1024,1024]{1,0:T(8,128)(2,1)} %get-tuple-element.9), channel_id=1, source_target_pairs={{0,8},{8,0},{16,24},{24,16},{1,9},{9,1},{17,25},{25,17},{2,10},{10... | collective-permute-start | bytes 6291464 | tf_op jit(solution)/shard_map/ppermute | solution.py:29
  362.5 52.2 %all-to-all-start.1 = ((bf16[8,64,1024]{2,1,0:T(8,128)(2,1)}), bf16[8,64,1024]{2,1,0:T(8,128)(2,1)S(1)}, u32[]{:S(2)}, u32[]{:S(2)}) async-start(bf16[8,64,1024]{2,1,0:T(8,128)(2,1)} %bitcast.9), calls=%async_computation.1 | async-start | bytes 2097152 | tf_op jit(solution)/shard_map/all_to_all | solution.py:64
  366.6 32.9 %copy-start = (f32[1024,1024]{1,0:T(8,128)S(1)}, f32[1024,1024]{1,0:T(8,128)}, u32[]{:S(2)}) copy-start(f32[1024,1024]{1,0:T(8,128)} %get-tuple-element.3) | copy-start | bytes 12582916
  366.6 32.9 %copy-start.1 = (f32[1024,1024]{1,0:T(8,128)S(1)}, f32[1024,1024]{1,0:T(8,128)}, u32[]{:S(2)}) copy-start(f32[1024,1024]{1,0:T(8,128)} %get-tuple-element.4) | copy-start | bytes 12582916
  366.6 32.9 %copy-start.2 = (f32[1,512,1024]{2,1,0:T(8,128)S(1)}, f32[1,512,1024]{2,1,0:T(8,128)}, u32[]{:S(2)}) copy-start(f32[1,512,1024]{2,1,0:T(8,128)} %param.10) | copy-start | bytes 6291460
Sparse Core Ops, SparseCore 0:
  9.5 109.1 all-gather.3
  120.3 209.8 all-gather.5
